TPU v7x, 32 devices: a whole 2x2x4 slice. The times are simulated.
32 devices in a mesh: groups: 2 (over y), cand: 4 (over z), tgt: 2 (over x), mix: 2 (over core).
Axes of the slice: x: 2, y: 2, z: 4, core: 2. Of those that a mesh axis runs over, the one named last changes fastest.
Arguments:
- candidates: bfloat16 [8192, 1024], P(('groups', 'cand')), parts along dimension 0, may hold values from -6 to 6
- targets: bfloat16 [4096, 1024], P(('groups', 'tgt')), parts along dimension 0, may hold values from -6 to 6
- member: int32 [4096], P('groups'), parts along dimension 0, may hold values from 0 to 15
- mix_weight: float32 [64, 32], P('mix', 'groups'), parts along dimension 1, may hold values from 0.1 to 10
Outputs:
- cand_potential: float32 [64, 8192], P('mix', ('groups', 'cand')), parts along dimension 1
- tgt_potential: float32 [64, 4096], P('mix', ('groups', 'tgt')), parts along dimension 1
There are 2 independent parts, one for each index of `groups`. A program takes and returns all parts, laid end to end along the dimension named above; each array names one. Nothing has to cross between parts.
All inputs are finite; a program needn't handle non-finite values.
Results may differ from a plain program's by a relative error of at most 0.0023.
Values sent between devices are 32-bit elements; how exact they have to be, the bound alone decides.
A program may use at most 64 MiB of HBM per device.

v0:
```python
import math
import jax
import jax.numpy as jnp
from jax import lax
from jax.sharding import PartitionSpec as P

ITERS = 2
EPS_FIRST = 0.05
EPS_SECOND = 0.025


def unit_rows(embedding):
    values = embedding.astype(jnp.float32)
    mean_sq = jnp.mean(values * values, axis=1, keepdims=True)
    return (values * lax.rsqrt(mean_sq + 1e-06) * (1.0 / math.sqrt(values.shape[1]))).astype(
        jnp.bfloat16
    )


def contract_last(left, right):
    return lax.dot_general(
        left, right, (((1,), (1,)), ((), ())), preferred_element_type=jnp.float32
    )


def target_mass(own_member, member, mix_weight, cand_total):
    task_ids = jnp.arange(mix_weight.shape[1], dtype=jnp.int32)
    counts = jnp.sum((member[None, :] == task_ids[:, None]).astype(jnp.float32), axis=1)
    weight_total = jnp.dot(mix_weight, counts, precision=lax.Precision.HIGHEST)
    onehot = (own_member[None, :] == task_ids[:, None]).astype(jnp.float32)
    per_target = jnp.dot(mix_weight, onehot, precision=lax.Precision.HIGHEST)
    return per_target * (cand_total / weight_total)[:, None]


def local(candidates, targets, member, mix_weight):
    cand_rows = candidates.shape[0]
    tgt_rows = targets.shape[0]
    tgt_total = tgt_rows * lax.axis_size("tgt")
    cand_total = cand_rows * lax.axis_size("cand")
    tgt_unit = unit_rows(targets)
    scores = contract_last(unit_rows(candidates), tgt_unit)
    own_member = lax.dynamic_slice_in_dim(member, lax.axis_index("tgt") * tgt_rows, tgt_rows, 0)
    mass = target_mass(own_member, member, mix_weight, float(cand_total))
    kernel_one = jnp.exp(scores / EPS_FIRST) / tgt_total
    kernel_two = jnp.exp(scores / EPS_SECOND) / tgt_total
    scale_tgt = jnp.ones((mix_weight.shape[0], tgt_rows), jnp.float32)
    scale_cand = jnp.ones((mix_weight.shape[0], cand_rows), jnp.float32)
    for section_index, kernel in enumerate((kernel_one, kernel_two)):
        if section_index == 1:
            scale_tgt = scale_tgt * scale_tgt
        for repeat in range(ITERS):
            partial_value = lax.dot_general(
                scale_tgt, kernel, (((1,), (1,)), ((), ())), precision=lax.Precision.HIGHEST
            )
            scale_cand = 1.0 / lax.psum(partial_value, "tgt")
            column_part = jnp.dot(scale_cand, kernel, precision=lax.Precision.HIGHEST)
            share_cols = tgt_rows // lax.axis_size("cand")
            summed = lax.psum_scatter(column_part, "cand", scatter_dimension=1, tiled=True)
            own_mass = lax.dynamic_slice_in_dim(
                mass, lax.axis_index("cand") * share_cols, share_cols, 1
            )
            scale_tgt = lax.all_gather(own_mass / summed, "cand", axis=1, tiled=True)
    return (jnp.log(scale_cand), jnp.log(scale_tgt))


def solution(mesh):
    in_specs = (
        P(("groups", "cand"), None),
        P(("groups", "tgt"), None),
        P("groups"),
        P("mix", "groups"),
    )
    out_specs = (P("mix", ("groups", "cand")), P("mix", ("groups", "tgt")))
    return jax.shard_map(local, mesh=mesh, in_specs=in_specs, out_specs=out_specs, check_vma=False)
```

profile of v0, /device:TPU:0, one launch (start us, length us, event | category | flops | bytes accessed | tf_op | source)
XLA Modules:
  0.0 290.6 jit_solution(8294371134683162558)
XLA Ops:
  7.2 2.2 fusion
  9.5 2.1 fusion.3
  11.6 2.5 fusion.6
  14.1 1.9 copy-done.1
  16.0 4.6 %fusion.15 = f32[32,1024]{1,0:T(8,128)} fusion(f32[1024,1024]{1,0:T(8,128)S(1)} %fusion.6), kind=kOutput, calls=%fused_computation.19 | convolution fusion | flops 404750336 | bytes 4325376 | tf_op jit(solution)/shard_map/dot_general | solution.py:52
  20.9 24.1 %all-reduce.5.cloned.1.call-done = f32[32,1024]{1,0:T(8,128)} async-done(((f32[32,1024]{1,0:T(8,128)}), f32[32,1024]{1,0:T(8,128)}) %all-reduce.5.cloned.1.call-update) | async-done | bytes 131088 | tf_op jit(solution)/shard_map/psum | solution.py:55
  45.0 5.9 %fusion.14 = f32[32,1024]{1,0:T(8,128)} fusion(f32[1024,1024]{1,0:T(8,128)} %copy-done.1, f32[32,1024]{1,0:T(8,128)} %all-reduce.5.cloned.1.call-done), kind=kOutput, calls=%fused_computation.18 | convolution fusion | flops 404783104 | bytes 4456448 | tf_op jit(solution)/shard_map/dot_general | solution.py:56
  51.1 0.3 fusion.29
  51.3 18.9 %reduce-scatter.5.cloned.1.call-done = f32[32,256]{1,0:T(8,128)} async-done(((f32[32,1024]{1,0:T(8,128)}), f32[32,256]{1,0:T(8,128)}) %reduce-scatter.5.cloned.1.call-update) | async-done | bytes 32784 | tf_op jit(solution)/shard_map/reduce_scatter | solution.py:58
  70.2 0.8 fusion.36
  71.0 13.6 %all_gather.12 = f32[32,1024]{1,0:T(8,128)S(1)} all-gather(f32[32,256]{1,0:T(8,128)S(1)} %fusion.36), channel_id=1, replica_groups=mesh['groups'=2,'cand'=4,'tgt'=2,'mix'=2] {'cand'}, dimensions={1}, use_global_device_ids=true | all-gather | bytes 163840 | tf_op jit(solution)/shard_map/all_gather | solution.py:62
  84.6 6.9 %fusion.13 = f32[32,1024]{1,0:T(8,128)} fusion(f32[32,1024]{1,0:T(8,128)S(1)} %all_gather.12, f32[1024,1024]{1,0:T(8,128)} %copy-done.1), kind=kOutput, calls=%fused_computation.17 | convolution fusion | flops 404750336 | bytes 4456448 | tf_op jit(solution)/shard_map/dot_general | solution.py:52
  91.6 19.7 %all-reduce.7.cloned.1.call-done = f32[32,1024]{1,0:T(8,128)} async-done(((f32[32,1024]{1,0:T(8,128)}), f32[32,1024]{1,0:T(8,128)}) %all-reduce.7.cloned.1.call-update) | async-done | bytes 131088 | tf_op jit(solution)/shard_map/psum | solution.py:55
  111.3 5.9 %fusion.12 = f32[32,1024]{1,0:T(8,128)} fusion(f32[1024,1024]{1,0:T(8,128)} %copy-done.1, f32[32,1024]{1,0:T(8,128)} %all-reduce.7.cloned.1.call-done), kind=kOutput, calls=%fused_computation.16 | convolution fusion | flops 404783104 | bytes 4456448 | tf_op jit(solution)/shard_map/dot_general | solution.py:56
  117.2 19.3 %reduce-scatter.7.cloned.1.call-done = f32[32,256]{1,0:T(8,128)} async-done(((f32[32,1024]{1,0:T(8,128)}), f32[32,256]{1,0:T(8,128)}) %reduce-scatter.7.cloned.1.call-update) | async-done | bytes 32784 | tf_op jit(solution)/shard_map/reduce_scatter | solution.py:58
  136.5 0.8 fusion.35
  137.4 13.4 %all_gather.13 = f32[32,1024]{1,0:T(8,128)S(1)} all-gather(f32[32,256]{1,0:T(8,128)S(1)} %fusion.35), channel_id=1, replica_groups=mesh['groups'=2,'cand'=4,'tgt'=2,'mix'=2] {'cand'}, dimensions={1}, use_global_device_ids=true | all-gather | bytes 163840 | tf_op jit(solution)/shard_map/all_gather | solution.py:62
  150.7 6.9 %fusion.19 = f32[32,1024]{1,0:T(8,128)} fusion(f32[1024,1024]{1,0:T(8,128)} %copy-done.1, f32[32,1024]{1,0:T(8,128)S(1)} %all_gather.13), kind=kOutput, calls=%fused_computation.23 | convolution fusion | flops 404783104 | bytes 4456448 | tf_op jit(solution)/shard_map/dot_general | solution.py:52
  157.7 0.3 reduce-scatter.9.cloned.1.call-start
  158.0 19.5 %all-reduce.9.cloned.1.call-done = f32[32,1024]{1,0:T(8,128)} async-done(((f32[32,1024]{1,0:T(8,128)}), f32[32,1024]{1,0:T(8,128)}) %all-reduce.9.cloned.1.call-update) | async-done | bytes 131088 | tf_op jit(solution)/shard_map/psum | solution.py:55
  177.5 5.9 %fusion.18 = f32[32,1024]{1,0:T(8,128)} fusion(f32[1024,1024]{1,0:T(8,128)} %copy-done.1, f32[32,1024]{1,0:T(8,128)} %all-reduce.9.cloned.1.call-done), kind=kOutput, calls=%fused_computation.22 | convolution fusion | flops 404783104 | bytes 4456448 | tf_op jit(solution)/shard_map/dot_general | solution.py:56
  183.4 19.3 %reduce-scatter.9.cloned.1.call-done = f32[32,256]{1,0:T(8,128)} async-done(((f32[32,1024]{1,0:T(8,128)}), f32[32,256]{1,0:T(8,128)}) %reduce-scatter.9.cloned.1.call-update) | async-done | bytes 32784 | tf_op jit(solution)/shard_map/reduce_scatter | solution.py:58
  202.7 0.8 fusion.34
  203.5 13.4 %all_gather.14 = f32[32,1024]{1,0:T(8,128)S(1)} all-gather(f32[32,256]{1,0:T(8,128)S(1)} %fusion.34), channel_id=1, replica_groups=mesh['groups'=2,'cand'=4,'tgt'=2,'mix'=2] {'cand'}, dimensions={1}, use_global_device_ids=true | all-gather | bytes 163840 | tf_op jit(solution)/shard_map/all_gather | solution.py:62
  216.9 6.9 %fusion.17 = f32[32,1024]{1,0:T(8,128)} fusion(f32[32,1024]{1,0:T(8,128)S(1)} %all_gather.14, f32[1024,1024]{1,0:T(8,128)} %copy-done.1), kind=kOutput, calls=%fused_computation.21 | convolution fusion | flops 404750336 | bytes 4456448 | tf_op jit(solution)/shard_map/dot_general | solution.py:52
  223.9 19.7 %all-reduce.11.cloned.1.call-done = f32[32,1024]{1,0:T(8,128)} async-done(((f32[32,1024]{1,0:T(8,128)}), f32[32,1024]{1,0:T(8,128)}) %all-reduce.11.cloned.1.call-update) | async-done | bytes 131088 | tf_op jit(solution)/shard_map/psum | solution.py:55
  243.6 5.9 %fusion.16 = f32[32,1024]{1,0:T(8,128)} fusion(f32[1024,1024]{1,0:T(8,128)} %copy-done.1, f32[32,1024]{1,0:T(8,128)} %all-reduce.11.cloned.1.call-done), kind=kOutput, calls=%fused_computation.20 | convolution fusion | flops 404783104 | bytes 4456448 | tf_op jit(solution)/shard_map/dot_general | solution.py:56
  249.6 0.7 fusion.30
  250.3 18.6 %reduce-scatter.11.cloned.1.call-done = f32[32,256]{1,0:T(8,128)} async-done(((f32[32,1024]{1,0:T(8,128)}), f32[32,256]{1,0:T(8,128)}) %reduce-scatter.11.cloned.1.call-update) | async-done | bytes 32784 | tf_op jit(solution)/shard_map/reduce_scatter | solution.py:58
  268.9 0.8 fusion.33
  269.8 13.4 %all_gather.15 = f32[32,1024]{1,0:T(8,128)S(1)} all-gather(f32[32,256]{1,0:T(8,128)S(1)} %fusion.33), channel_id=1, replica_groups=mesh['groups'=2,'cand'=4,'tgt'=2,'mix'=2] {'cand'}, dimensions={1}, use_global_device_ids=true | all-gather | bytes 163840 | tf_op jit(solution)/shard_map/all_gather | solution.py:62
  283.1 0.7 log.7
  (30 shorter events, 0.7 us)
Async XLA Ops:
  7.2 43.8 %copy-start = (f32[32,16]{0,1:T(8,128)S(1)}, f32[32,16]{0,1:T(8,128)}, u32[]{:S(2)}) copy-start(f32[32,16]{0,1:T(8,128)} %param.7) | copy-start | bytes 6148
  7.2 4.4 %copy-start.2 = (bf16[1024,1024]{1,0:T(8,128)(2,1)S(1)}, bf16[1024,1024]{1,0:T(8,128)(2,1)}, u32[]{:S(2)}) copy-start(bf16[1024,1024]{1,0:T(8,128)(2,1)} %param.5) | copy-start | bytes 6291460
  7.2 37.8 %all-reduce.5.cloned.1.call-start = ((), (), s32[]{:S(2)}) async-start(), calls=%async_computation.4 | async-start | bytes 262144 | tf_op jit(solution)/shard_map/psum | solution.py:55
  7.2 4.3 %copy-start.3 = (bf16[1024,1024]{1,0:T(8,128)(2,1)S(1)}, bf16[1024,1024]{1,0:T(8,128)(2,1)}, u32[]{:S(2)}) copy-start(bf16[1024,1024]{1,0:T(8,128)(2,1)} %param.4) | copy-start | bytes 6291460
  14.1 1.9 copy-start.1
  16.0 4.7 %copy-start.5 = (s32[2048]{0:T(1024)S(1)}, s32[2048]{0:T(1024)}, u32[]{:S(2)}) copy-start(s32[2048]{0:T(1024)} %param.6) | copy-start | bytes 24580
  20.7 49.5 %reduce-scatter.5.cloned.1.call-start = ((), (), s32[]{:S(2)}) async-start(), calls=%async_computation.5 | async-start | bytes 163840 | tf_op jit(solution)/shard_map/reduce_scatter | solution.py:58
  50.9 60.4 %all-reduce.7.cloned.1.call-start = ((), (), s32[]{:S(2)}) async-start(), calls=%async_computation.6 | async-start | bytes 262144 | tf_op jit(solution)/shard_map/psum | solution.py:55
  91.5 45.0 %reduce-scatter.7.cloned.1.call-start = ((), (), s32[]{:S(2)}) async-start(), calls=%async_computation.7 | async-start | bytes 163840 | tf_op jit(solution)/shard_map/reduce_scatter | solution.py:58
  117.2 60.3 %all-reduce.9.cloned.1.call-start = ((), (), s32[]{:S(2)}) async-start(), calls=%async_computation.8 | async-start | bytes 262144 | tf_op jit(solution)/shard_map/psum | solution.py:55
  157.7 45.0 %reduce-scatter.9.cloned.1.call-start = ((), (), s32[]{:S(2)}) async-start(), calls=%async_computation.9 | async-start | bytes 163840 | tf_op jit(solution)/shard_map/reduce_scatter | solution.py:58
  183.4 60.3 %all-reduce.11.cloned.1.call-start = ((), (), s32[]{:S(2)}) async-start(), calls=%async_computation.10 | async-start | bytes 262144 | tf_op jit(solution)/shard_map/psum | solution.py:55
  223.9 45.1 %reduce-scatter.11.cloned.1.call-start = ((), (), s32[]{:S(2)}) async-start(), calls=%async_computation.11 | async-start | bytes 163840 | tf_op jit(solution)/shard_map/reduce_scatter | solution.py:58
  243.6 5.9 %copy-start.4 = (f32[32,1024]{1,0:T(8,128)S(1)}, f32[32,1024]{1,0:T(8,128)}, u32[]{:S(2)}) copy-start(f32[32,1024]{1,0:T(8,128)} %all-reduce.11.cloned.1.call-done) | copy-start | bytes 393220
Sparse Core Ops, SparseCore 0:
  20.8 24.0 all-reduce.4
  51.0 19.1 reduce-scatter.4
  91.7 19.5 all-reduce.6
  117.3 19.1 reduce-scatter.6
  157.8 19.6 all-reduce.8
  183.5 19.1 reduce-scatter.8
  224.0 19.6 all-reduce.10
  249.7 19.1 reduce-scatter.10
where the time goes:
time: 291 us
  waiting for transfers between devices  159 us (55%)
  blocking collectives  53.7 us (18%)
  matrix products  51.8 us (18%)
  between operations  14.2 us (5%)
  other arithmetic  8.44 us (3%)
    psum x4, waiting for transfers between devices, local(): scale_cand = 1.0 / lax.psum(partial_value, 'tgt')  83 us
    reduce_scatter x4, waiting for transfers between devices, local(): lax.psum_scatter(column_part, 'cand', scatter_dimension=1, tiled=True)  76.1 us
    all_gather x4, blocking collectives, local(): scale_tgt = lax.all_gather(own_mass / summed, 'cand', axis=1, tiled=True)  53.7 us
    dot_general x4, matrix products, local(): lax.dot_general(scale_tgt, kernel, (((1,), (1,)), ((), ())), precision=la...  25.4 us
    dot_general x4, matrix products, local(): column_part = jnp.dot(scale_cand, kernel, precision=lax.Precision.HIGHEST)  23.5 us
  transfers between devices with their start and end apart: 8, of which 8 were waited for; matrix products, arithmetic and copies ran while one was open for 0% of the time, Pallas kernels for 0%

commit v1 on v0

--- a/solution.py
+++ b/solution.py
@@ -52,7 +52,7 @@
             partial_value = lax.dot_general(
                 scale_tgt, kernel, (((1,), (1,)), ((), ())), precision=lax.Precision.HIGHEST
             )
-            scale_cand = 1.0 / lax.psum(partial_value, "tgt")
+            scale_cand = 1.0 / jnp.sum(lax.all_gather(partial_value, "tgt"), axis=0)
             column_part = jnp.dot(scale_cand, kernel, precision=lax.Precision.HIGHEST)
             share_cols = tgt_rows // lax.axis_size("cand")
             summed = lax.psum_scatter(column_part, "cand", scatter_dimension=1, tiled=True)

time: 291 us -> 225 us (0.77)
  waiting for transfers between devices: 159 us -> 72.2 us
  blocking collectives: 53.7 us -> 77.9 us
  matrix products: 51.8 us -> 48.8 us
    psum x4 -> x0, waiting for transfers between devices: 83 us -> none  [local(): scale_cand = 1.0 / lax.psum(partial_value, 'tgt')]
    all_gather x0 -> x4, blocking collectives: none -> 24.2 us  [local(): scale_cand = 1.0 / jnp.sum(lax.all_gather(partial_value, 'tgt'), axis=0)]
    reduce_scatter x4, waiting for transfers between devices: 76.1 us -> 72.2 us  [local(): lax.psum_scatter(column_part, 'cand', scatter_dimension=1, tiled=True)]
  transfers between devices with their start and end apart: 8 -> 4, of which waited for: 8 -> 4; matrix products, arithmetic and copies ran while one was open for 0% -> 1% of each run, Pallas kernels for 0% -> 0%
where the time goes in v1:
time: 225 us; the launch traced here: 224 us
  blocking collectives  77.9 us (35%)
  waiting for transfers between devices  72.2 us (32%)
  matrix products  48.8 us (22%)
  between operations  13.9 us (6%)
  other arithmetic  8.51 us (4%)
  local copies, waits for them, and re-layouts  2.62 us (1%)
    reduce_scatter x4, waiting for transfers between devices, local(): lax.psum_scatter(column_part, 'cand', scatter_dimension=1, tiled=True)  72.2 us
    all_gather x4, blocking collectives, local(): scale_tgt = lax.all_gather(own_mass / summed, 'cand', axis=1, tiled=True)  53.7 us
    all_gather x4, blocking collectives, local(): scale_cand = 1.0 / jnp.sum(lax.all_gather(partial_value, 'tgt'), axis=0)  24.2 us
    dot_general x4, matrix products, local(): column_part = jnp.dot(scale_cand, kernel, precision=lax.Precision.HIGHEST)  23.2 us
    dot_general x4, matrix products, local(): lax.dot_general(scale_tgt, kernel, (((1,), (1,)), ((), ())), precision=la...  22.7 us
  transfers between devices with their start and end apart: 4, of which 4 were waited for; matrix products, arithmetic and copies ran while one was open for 1% of the time, Pallas kernels for 0%

profile of v1, /device:TPU:0, one launch (start us, length us, event | category | flops | bytes accessed | tf_op | source)
XLA Modules:
  0.0 224.2 jit_solution(10759214154046182691)
XLA Ops:
  7.2 2.2 fusion
  9.5 2.1 fusion.3
  11.6 2.5 %fusion.6 = f32[1024,1024]{1,0:T(8,128)S(1)} fusion(bf16[1024,1024]{1,0:T(8,128)(2,1)S(1)} %copy-done.2, bf16[1024,1024]{1,0:T(8,128)(2,1)S(1)} %copy-done.3, f32[1024]{0:T(1024)S(1)} %get-tuple-element.2, f32[1024]{0:T(1024)S(1)} %get-tuple-element.3), kind=kOutput, calls=%fused_computation.12 | convolution fusion | flops 2155872256 | bytes 8396800 | tf_op jit(solution)/shard_map/dot_general | solution.py:21
  14.1 1.9 copy-done.1
  16.0 4.0 %fusion.15 = f32[32,1024]{1,0:T(8,128)S(1)} fusion(f32[1024,1024]{1,0:T(8,128)S(1)} %fusion.6), kind=kOutput, calls=%fused_computation.19 | convolution fusion | flops 404750336 | bytes 4325376 | tf_op jit(solution)/shard_map/dot_general | solution.py:52
  20.0 7.1 %all-gather = f32[64,1024]{1,0:T(8,128)S(1)} all-gather(f32[32,1024]{1,0:T(8,128)S(1)} %fusion.15), channel_id=2, replica_groups=mesh['groups'=2,'cand'=4,'tgt'=2,'mix'=2] {'tgt'}, dimensions={0}, use_global_device_ids=true | all-gather | bytes 393216 | tf_op jit(solution)/shard_map/all_gather | solution.py:55
  27.1 5.8 %fusion.14 = f32[32,1024]{1,0:T(8,128)} fusion(f32[1024,1024]{1,0:T(8,128)} %copy-done.1, f32[32,1024]{1,0:T(8,128)S(1)} %reduce_sum.66), kind=kOutput, calls=%fused_computation.18 | convolution fusion | flops 404783104 | bytes 4456448 | tf_op jit(solution)/shard_map/dot_general | solution.py:56
  33.0 0.1 convert_reduce_fusion
  33.3 0.3 fusion.29
  33.6 20.3 %reduce-scatter.5.cloned.1.call-done = f32[32,256]{1,0:T(8,128)} async-done(((f32[32,1024]{1,0:T(8,128)}), f32[32,256]{1,0:T(8,128)}) %reduce-scatter.5.cloned.1.call-update) | async-done | bytes 32784 | tf_op jit(solution)/shard_map/reduce_scatter | solution.py:58
  53.8 0.8 fusion.36
  54.7 13.5 %all_gather.38 = f32[32,1024]{1,0:T(8,128)S(1)} all-gather(f32[32,256]{1,0:T(8,128)S(1)} %fusion.36), channel_id=1, replica_groups=mesh['groups'=2,'cand'=4,'tgt'=2,'mix'=2] {'cand'}, dimensions={1}, use_global_device_ids=true | all-gather | bytes 163840 | tf_op jit(solution)/shard_map/all_gather | solution.py:62
  68.2 6.2 %fusion.13 = f32[32,1024]{1,0:T(8,128)S(1)} fusion(f32[32,1024]{1,0:T(8,128)S(1)} %all_gather.38, f32[1024,1024]{1,0:T(8,128)} %copy-done.1), kind=kOutput, calls=%fused_computation.17 | convolution fusion | flops 404750336 | bytes 4456448 | tf_op jit(solution)/shard_map/dot_general | solution.py:52
  74.5 5.6 %all-gather.1 = f32[64,1024]{1,0:T(8,128)S(1)} all-gather(f32[32,1024]{1,0:T(8,128)S(1)} %fusion.13), channel_id=3, replica_groups=mesh['groups'=2,'cand'=4,'tgt'=2,'mix'=2] {'tgt'}, dimensions={0}, use_global_device_ids=true | all-gather | bytes 393216 | tf_op jit(solution)/shard_map/all_gather | solution.py:55
  80.1 5.8 %fusion.12 = f32[32,1024]{1,0:T(8,128)} fusion(f32[1024,1024]{1,0:T(8,128)} %copy-done.1, f32[32,1024]{1,0:T(8,128)S(1)} %reduce_sum.67), kind=kOutput, calls=%fused_computation.16 | convolution fusion | flops 404783104 | bytes 4456448 | tf_op jit(solution)/shard_map/dot_general | solution.py:56
  86.0 17.5 %reduce-scatter.7.cloned.1.call-done = f32[32,256]{1,0:T(8,128)} async-done(((f32[32,1024]{1,0:T(8,128)}), f32[32,256]{1,0:T(8,128)}) %reduce-scatter.7.cloned.1.call-update) | async-done | bytes 32784 | tf_op jit(solution)/shard_map/reduce_scatter | solution.py:58
  103.5 0.8 fusion.35
  104.4 13.4 %all_gather.41 = f32[32,1024]{1,0:T(8,128)S(1)} all-gather(f32[32,256]{1,0:T(8,128)S(1)} %fusion.35), channel_id=1, replica_groups=mesh['groups'=2,'cand'=4,'tgt'=2,'mix'=2] {'cand'}, dimensions={1}, use_global_device_ids=true | all-gather | bytes 163840 | tf_op jit(solution)/shard_map/all_gather | solution.py:62
  117.7 6.2 %fusion.19 = f32[32,1024]{1,0:T(8,128)S(1)} fusion(f32[1024,1024]{1,0:T(8,128)} %copy-done.1, f32[32,1024]{1,0:T(8,128)S(1)} %all_gather.41), kind=kOutput, calls=%fused_computation.23 | convolution fusion | flops 404783104 | bytes 4456448 | tf_op jit(solution)/shard_map/dot_general | solution.py:52
  124.0 5.9 %all-gather.2 = f32[64,1024]{1,0:T(8,128)S(1)} all-gather(f32[32,1024]{1,0:T(8,128)S(1)} %fusion.19), channel_id=4, replica_groups=mesh['groups'=2,'cand'=4,'tgt'=2,'mix'=2] {'tgt'}, dimensions={0}, use_global_device_ids=true | all-gather | bytes 393216 | tf_op jit(solution)/shard_map/all_gather | solution.py:55
  129.9 5.8 %fusion.18 = f32[32,1024]{1,0:T(8,128)} fusion(f32[1024,1024]{1,0:T(8,128)} %copy-done.1, f32[32,1024]{1,0:T(8,128)S(1)} %reduce_sum.68), kind=kOutput, calls=%fused_computation.22 | convolution fusion | flops 404783104 | bytes 4456448 | tf_op jit(solution)/shard_map/dot_general | solution.py:56
  135.7 17.5 %reduce-scatter.9.cloned.1.call-done = f32[32,256]{1,0:T(8,128)} async-done(((f32[32,1024]{1,0:T(8,128)}), f32[32,256]{1,0:T(8,128)}) %reduce-scatter.9.cloned.1.call-update) | async-done | bytes 32784 | tf_op jit(solution)/shard_map/reduce_scatter | solution.py:58
  153.2 0.8 fusion.34
  154.1 13.4 %all_gather.44 = f32[32,1024]{1,0:T(8,128)S(1)} all-gather(f32[32,256]{1,0:T(8,128)S(1)} %fusion.34), channel_id=1, replica_groups=mesh['groups'=2,'cand'=4,'tgt'=2,'mix'=2] {'cand'}, dimensions={1}, use_global_device_ids=true | all-gather | bytes 163840 | tf_op jit(solution)/shard_map/all_gather | solution.py:62
  167.5 6.2 %fusion.17 = f32[32,1024]{1,0:T(8,128)S(1)} fusion(f32[32,1024]{1,0:T(8,128)S(1)} %all_gather.44, f32[1024,1024]{1,0:T(8,128)} %copy-done.1), kind=kOutput, calls=%fused_computation.21 | convolution fusion | flops 404750336 | bytes 4456448 | tf_op jit(solution)/shard_map/dot_general | solution.py:52
  173.7 5.6 %all-gather.3 = f32[64,1024]{1,0:T(8,128)S(1)} all-gather(f32[32,1024]{1,0:T(8,128)S(1)} %fusion.17), channel_id=5, replica_groups=mesh['groups'=2,'cand'=4,'tgt'=2,'mix'=2] {'tgt'}, dimensions={0}, use_global_device_ids=true | all-gather | bytes 393216 | tf_op jit(solution)/shard_map/all_gather | solution.py:55
  179.4 5.8 %fusion.16 = f32[32,1024]{1,0:T(8,128)} fusion(f32[1024,1024]{1,0:T(8,128)} %copy-done.1, f32[32,1024]{1,0:T(8,128)S(1)} %reduce_sum.69), kind=kOutput, calls=%fused_computation.20 | convolution fusion | flops 404783104 | bytes 4456448 | tf_op jit(solution)/shard_map/dot_general | solution.py:56
  185.2 0.7 fusion.30
  185.9 16.9 %reduce-scatter.11.cloned.1.call-done = f32[32,256]{1,0:T(8,128)} async-done(((f32[32,1024]{1,0:T(8,128)}), f32[32,256]{1,0:T(8,128)}) %reduce-scatter.11.cloned.1.call-update) | async-done | bytes 32784 | tf_op jit(solution)/shard_map/reduce_scatter | solution.py:58
  202.8 0.8 fusion.33
  203.6 13.4 %all_gather.47 = f32[32,1024]{1,0:T(8,128)S(1)} all-gather(f32[32,256]{1,0:T(8,128)S(1)} %fusion.33), channel_id=1, replica_groups=mesh['groups'=2,'cand'=4,'tgt'=2,'mix'=2] {'cand'}, dimensions={1}, use_global_device_ids=true | all-gather | bytes 163840 | tf_op jit(solution)/shard_map/all_gather | solution.py:62
  217.0 0.7 log.7
  (24 shorter events, 0.5 us)
Async XLA Ops:
  7.2 26.0 %copy-start = (f32[32,16]{0,1:T(8,128)S(1)}, f32[32,16]{0,1:T(8,128)}, u32[]{:S(2)}) copy-start(f32[32,16]{0,1:T(8,128)} %param.7) | copy-start | bytes 6148
  7.2 4.4 %copy-start.2 = (bf16[1024,1024]{1,0:T(8,128)(2,1)S(1)}, bf16[1024,1024]{1,0:T(8,128)(2,1)}, u32[]{:S(2)}) copy-start(bf16[1024,1024]{1,0:T(8,128)(2,1)} %param.5) | copy-start | bytes 6291460
  7.2 46.7 %reduce-scatter.5.cloned.1.call-start = ((), (), s32[]{:S(2)}) async-start(), calls=%async_computation.4 | async-start | bytes 163840 | tf_op jit(solution)/shard_map/reduce_scatter | solution.py:58
  7.2 4.3 %copy-start.3 = (bf16[1024,1024]{1,0:T(8,128)(2,1)S(1)}, bf16[1024,1024]{1,0:T(8,128)(2,1)}, u32[]{:S(2)}) copy-start(bf16[1024,1024]{1,0:T(8,128)(2,1)} %param.4) | copy-start | bytes 6291460
  14.1 1.9 copy-start.1
  16.0 17.0 %copy-start.4 = (s32[2048]{0:T(1024)S(1)}, s32[2048]{0:T(1024)}, u32[]{:S(2)}) copy-start(s32[2048]{0:T(1024)} %param.6) | copy-start | bytes 24580
  33.0 70.6 %reduce-scatter.7.cloned.1.call-start = ((), (), s32[]{:S(2)}) async-start(), calls=%async_computation.5 | async-start | bytes 163840 | tf_op jit(solution)/shard_map/reduce_scatter | solution.py:58
  86.0 67.3 %reduce-scatter.9.cloned.1.call-start = ((), (), s32[]{:S(2)}) async-start(), calls=%async_computation.6 | async-start | bytes 163840 | tf_op jit(solution)/shard_map/reduce_scatter | solution.py:58
  135.7 67.1 %reduce-scatter.11.cloned.1.call-start = ((), (), s32[]{:S(2)}) async-start(), calls=%async_computation.7 | async-start | bytes 163840 | tf_op jit(solution)/shard_map/reduce_scatter | solution.py:58
Sparse Core Ops, SparseCore 0:
  33.1 20.7 reduce-scatter.4
  86.1 17.3 reduce-scatter.6
  135.8 17.3 reduce-scatter.8
  185.3 17.3 reduce-scatter.10
